TPU v7x, 32 devices: a whole 2x2x4 slice. The times are simulated.
32 devices in a mesh: ch: 4 (over y, x), row: 8 (over z, core).
Axes of the slice: x: 2, y: 2, z: 4, core: 2. Of those that a mesh axis runs over, the one named last changes fastest.
Arguments:
- latent: bfloat16 [128, 32, 1280], P('row', None, 'ch'), may hold values from -50 to 50
- timestep: int32 [4], replicated, may hold values from 0 to 999
- norm_gain_a: float32 [1280], P('ch'), may hold values from 0.1 to 1.9
- conv_weight_a: bfloat16 [1280, 3, 3, 1280], P('ch'), may hold values from -0.0546875 to 0.0546875
- time_weight: bfloat16 [320, 1280], P(None, 'ch'), may hold values from -0.3125 to 0.3125
- norm_gain_b: float32 [1280], P('ch'), may hold values from 0.1 to 1.9
- conv_weight_b: bfloat16 [1280, 3, 3, 1280], P('ch'), may hold values from -0.0546875 to 0.0546875
- norm_gain_c: float32 [1280], P('ch'), may hold values from 0.1 to 1.9
- w_query: bfloat16 [1024, 1280], P('ch'), may hold values from -4 to 4
- w_key: bfloat16 [1024, 1280], P('ch'), may hold values from -4 to 4
- w_value: bfloat16 [1024, 1280], P('ch'), may hold values from -0.3125 to 0.3125
- w_out: bfloat16 [1280, 1024], P('ch'), may hold values from -0.1875 to 0.1875
Outputs:
- result: bfloat16 [128, 32, 1280], P('row', None, 'ch')
All inputs are finite; a program needn't handle non-finite values.
Results may differ from a plain program's by a relative error of at most 0.017.
Values may be sent and summed in bfloat16 or wider, within the bound.
A program may use at most 64 MiB of HBM per device.

v0:
```python
import math
import jax
import jax.numpy as jnp
from jax import lax
from jax.sharding import PartitionSpec as P

C = 1280
GROUPS = 32
HEAD_DIM = 64
TDIM = 320
H = 32
eps_value = 1e-06


def swapped(value, axis, stride):
    mask = 2**stride
    pairs = [(source, source ^ mask) for source in range(lax.axis_size(axis))]
    return lax.ppermute(value, axis, pairs)


def right_product(left, weight):
    return lax.dot_general(
        left, weight, (((1,), (1,)), ((), ())), preferred_element_type=jnp.float32
    )


def conv_taps(padded, weight):
    outcome = lax.conv_general_dilated(
        padded[None],
        weight,
        (1, 1),
        "VALID",
        dimension_numbers=("NHWC", "OHWI", "NHWC"),
        preferred_element_type=jnp.float32,
    )
    return outcome[0]


def pad_columns(field):
    return jnp.pad(field, ((0, 0), (1, 1), (0, 0)))


def body(
    latent,
    timestep,
    norm_gain_a,
    conv_weight_a,
    time_weight,
    norm_gain_b,
    conv_weight_b,
    norm_gain_c,
    w_query,
    w_key,
    w_value,
    w_out,
):
    rows, width, local_ch = latent.shape
    span = H // rows
    place = lax.axis_index("row")
    within = place % span
    image_id = place // span
    group_width = C // GROUPS
    local_groups = local_ch // group_width
    members = float(H * width * group_width)
    tokens = rows * width

    def group_norm(value, gain):
        flat = value.reshape(tokens, local_groups, group_width)
        stats = jnp.stack([jnp.sum(flat, axis=(0, 2)), jnp.sum(flat * flat, axis=(0, 2))])
        stats = stats + swapped(stats, "row", 0)
        mean = stats[0] / members
        spread = stats[1] / members - mean * mean
        scaled = (flat - mean[None, :, None]) * lax.rsqrt(spread + eps_value)[None, :, None]
        return scaled.reshape(rows, width, local_ch) * gain

    upper_half = within == 0

    def facing_row(field):
        return jnp.where(upper_half, field[-1:], field[:1])

    def attach_rim(field, partner):
        empty_row = jnp.zeros_like(partner)
        above = jnp.where(upper_half, empty_row, partner)
        below = jnp.where(upper_half, partner, empty_row)
        return jnp.concatenate([above, field, below], axis=0)

    def convolve(active, weight):
        full = lax.all_gather(active, "ch", axis=2, tiled=True)
        partner = swapped(facing_row(full), "row", 0)
        rimmed = attach_rim(full, partner)
        result_conv = conv_taps(pad_columns(rimmed), weight)
        return result_conv

    image_ids = jnp.arange(timestep.shape[0])
    step_value = jnp.sum(jnp.where(image_ids == image_id, timestep, 0)).astype(jnp.float32)
    half = TDIM // 2
    freqs = jnp.exp(-math.log(10000.0) * jnp.arange(half, dtype=jnp.float32) / half)
    angles = step_value * freqs
    sinus = jnp.concatenate([jnp.cos(angles), jnp.sin(angles)])[None, :].astype(jnp.bfloat16)
    time_add = jax.nn.silu(jnp.dot(sinus, time_weight, preferred_element_type=jnp.float32))
    source = latent.astype(jnp.float32)
    active_a = jax.nn.silu(group_norm(source, norm_gain_a)).astype(jnp.bfloat16)
    hidden_a = convolve(active_a, conv_weight_a) + time_add[None]
    active_b = jax.nn.silu(group_norm(hidden_a, norm_gain_b)).astype(jnp.bfloat16)
    hidden_b = source + convolve(active_b, conv_weight_b)
    normed = group_norm(hidden_b, norm_gain_c).astype(jnp.bfloat16).reshape(tokens, local_ch)
    inner = w_query.shape[0]
    projections = jnp.concatenate([w_query, w_key, w_value], axis=0)
    weight_cols = projections
    mixed = right_product(lax.all_gather(normed, "ch", axis=1, tiled=True), weight_cols)
    query = mixed[:, :inner].astype(jnp.bfloat16)
    keyed = mixed[:, inner : 2 * inner].astype(jnp.bfloat16)
    valued = mixed[:, 2 * inner :].astype(jnp.bfloat16)
    key_value = jnp.stack([keyed, valued])
    key_value = jnp.concatenate([key_value, swapped(key_value, "row", 0)], axis=1)
    local_heads = inner // HEAD_DIM
    query_heads = query.reshape(tokens, local_heads, HEAD_DIM)
    key_heads = key_value[0].reshape(-1, local_heads, HEAD_DIM)
    value_heads = key_value[1].reshape(-1, local_heads, HEAD_DIM)
    scores = jnp.einsum(
        "qhd,khd->hqk", query_heads, key_heads, preferred_element_type=jnp.float32
    ) * (1.0 / math.sqrt(HEAD_DIM))
    highest = jnp.max(scores, axis=-1, keepdims=True)
    raised = jnp.exp(scores - highest)
    weights = (raised / jnp.sum(raised, axis=-1, keepdims=True)).astype(jnp.bfloat16)
    heads_out = jnp.einsum("hqk,khd->qhd", weights, value_heads, preferred_element_type=jnp.float32)
    heads_out = heads_out.astype(jnp.bfloat16).reshape(tokens, inner)
    weight_cols = w_out
    projected = right_product(lax.all_gather(heads_out, "ch", axis=1, tiled=True), weight_cols)
    total = hidden_b.reshape(tokens, local_ch) + projected
    return total.reshape(rows, width, local_ch).astype(jnp.bfloat16)


def solution(mesh):
    return jax.shard_map(
        body,
        mesh=mesh,
        in_specs=(
            P("row", None, "ch"),
            P(),
            P("ch"),
            P("ch", None, None, None),
            P(None, "ch"),
            P("ch"),
            P("ch", None, None, None),
            P("ch"),
            P("ch", None),
            P("ch", None),
            P("ch", None),
            P("ch", None),
        ),
        out_specs=P("row", None, "ch"),
        check_vma=False,
    )
```

profile of v0, /device:TPU:0, one launch (start us, length us, event | category | flops | bytes accessed | tf_op | source)
XLA Modules:
  0.0 277.8 jit_solution(7291214916432832792)
XLA Ops:
  6.5 1.3 convert_reduce_fusion
  9.9 1.3 fusion.55
  11.2 1.8 copy.96
  14.7 62.4 %all-gather.5.cloned.1.call-done = bf16[16,32,1280]{1,0,2:T(8,128)(2,1)} async-done(((bf16[16,32,320]{1,0,2:T(8,128)(2,1)}), bf16[16,32,1280]{1,0,2:T(8,128)(2,1)}) %all-gather.5.cloned.1.call-update) | async-done | bytes 1310736 | tf_op jit(solution)/shard_map/all_gather | solution.py:88
  77.1 3.0 %broadcast_select_fusion.5 = bf16[1,32,1280]{1,0,2:T(2,128)(2,1)S(1)} fusion(pred[]{:T(512)S(6)} %eq.11, bf16[16,32,1280]{1,0,2:T(8,128)(2,1)} %all-gather.5.cloned.1.call-done), kind=kLoop, calls=%fused_computation.48 | loop fusion | flops 40960 | bytes 245761 | tf_op jit(solution)/shard_map/jit(_where)/select_n | solution.py:79
  80.6 6.0 %copy.101 = bf16[16,32,1280]{2,1,0:T(8,128)(2,1)S(1)} copy(bf16[16,32,1280]{1,0,2:T(8,128)(2,1)} %all-gather.5.cloned.1.call-done) | data formatting | bytes 2621440 | tf_op jit(solution)/shard_map/all_gather | solution.py:88
  87.1 1.9 broadcast_select_fusion.4
  89.0 1.3 copy.100
  92.3 1.1 slice-done
  94.5 7.8 %select_reduce_fusion.1 = (f32[320]{0:T(512)S(1)}, f32[320]{0:T(512)S(1)}, f32[16,8,5,320]{3,1,2,0:T(8,128)S(1)}) fusion(f32[320]{0:T(512)S(1)} %divide_multiply_fusion, pred[8,5]{0,1:T(8,128)(4,1)S(1)} %copy-done.8, bf16[320,3,3,1280]{3,0,2,1:T(8,128)(2,1)S(1)} %bitcast.121, bf16[18,1,7,2,1280]{4,2,3,0,1:T(8,128)(2,1)S(1)} %slice.69, ...), kind=kOutput, calls=%fused_computation.59 | convolution fusion | flops 4727766016 | bytes 10684200 | tf_op jit(solution)/shard_map/conv_general_dilated | solution.py:28
  104.8 2.0 copy.107
  106.8 61.4 %all-gather.7.cloned.1.call-done = bf16[16,32,1280]{1,0,2:T(8,128)(2,1)} async-done(((bf16[16,32,320]{1,0,2:T(8,128)(2,1)}), bf16[16,32,1280]{1,0,2:T(8,128)(2,1)}) %all-gather.7.cloned.1.call-update) | async-done | bytes 1310736 | tf_op jit(solution)/shard_map/all_gather | solution.py:88
  168.2 3.0 %broadcast_select_fusion.2 = bf16[1,32,1280]{1,0,2:T(2,128)(2,1)S(1)} fusion(pred[]{:T(512)S(6)} %eq.11, bf16[16,32,1280]{1,0,2:T(8,128)(2,1)} %all-gather.7.cloned.1.call-done), kind=kLoop, calls=%fused_computation.45 | loop fusion | flops 40960 | bytes 245761 | tf_op jit(solution)/shard_map/jit(_where)/select_n | solution.py:79
  171.7 6.0 %copy.112 = bf16[16,32,1280]{2,1,0:T(8,128)(2,1)S(1)} copy(bf16[16,32,1280]{1,0,2:T(8,128)(2,1)} %all-gather.7.cloned.1.call-done) | data formatting | bytes 2621440 | tf_op jit(solution)/shard_map/all_gather | solution.py:88
  178.2 1.9 broadcast_select_fusion.1
  180.1 1.3 copy.111
  185.6 7.8 %fusion.35 = f32[16,8,5,320]{3,1,2,0:T(8,128)S(1)} fusion(bf16[320,3,3,1280]{3,0,2,1:T(8,128)(2,1)S(1)} %bitcast.123, bf16[18,1,7,2,1280]{4,2,3,0,1:T(8,128)(2,1)S(1)} %slice.73, bf16[18,1,8,5,1280]{4,2,3,0,1:T(8,128)(2,1)S(1)} %copy.116, pred[8,5]{0,1:T(8,128)(4,1)S(1)} %copy-done.8), kind=kOutput, calls=%fused_computation.49 | convolution fusion | flops 4726538240 | bytes 10680360 | tf_op jit(solution)/shard_map/conv_general_dilated | solution.py:28
  197.2 28.8 %all-gather.9.cloned.1.call-done = bf16[512,1280]{0,1:T(8,128)(2,1)} async-done(((bf16[512,320]{0,1:T(8,128)(2,1)}), bf16[512,1280]{0,1:T(8,128)(2,1)}) %all-gather.9.cloned.1.call-update) | async-done | bytes 1310736 | tf_op jit(solution)/shard_map/all_gather | solution.py:110
  225.9 2.7 fusion.32
  229.0 1.7 collective-permute-done.5
  231.3 5.0 %fusion.81 = (f32[4,512]{1,0:T(4,128)S(1)}, f32[4,512,1024]{2,1,0:T(8,128)}) fusion(bf16[512,4,64]{0,2,1:T(8,128)(2,1)S(1)} %bitcast.106, bf16[1024,4,64]{0,2,1:T(8,128)(2,1)S(1)} %bitcast.104), kind=kOutput, calls=%fused_computation.118 | convolution fusion | flops 274727936 | bytes 9183232 | tf_op jit(solution)/shard_map/sub | solution.py:124
  236.4 5.5 %fusion.44 = bf16[4,64,512]{2,1,0:T(8,128)(2,1)} fusion(bf16[1024,4,64]{0,2,1:T(8,128)(2,1)S(1)} %bitcast.105, f32[4,512,1024]{2,1,0:T(8,128)} %get-tuple-element.23, f32[4,512]{1,0:T(4,128)S(1)} %get-tuple-element.22), kind=kOutput, calls=%fused_computation.55 | convolution fusion | flops 272760832 | bytes 9183232 | tf_op jit(solution)/shard_map/hqk,khd->qhd/dot_general | solution.py:126
  242.5 26.1 %all-gather.11.cloned.1.call-done = bf16[512,1024]{0,1:T(8,128)(2,1)} async-done(((bf16[512,256]{0,1:T(8,128)(2,1)}), bf16[512,1024]{0,1:T(8,128)(2,1)}) %all-gather.11.cloned.1.call-update) | async-done | bytes 1048592 | tf_op jit(solution)/shard_map/all_gather | solution.py:129
  268.6 1.7 fusion.43
  (121 shorter events, 20.7 us)
Async XLA Ops:
  6.5 262.1 %copy-start = (bf16[320,1024]{1,0:T(8,128)(2,1)S(1)}, bf16[320,1024]{1,0:T(8,128)(2,1)}, u32[]{:S(2)}) copy-start(bf16[320,1024]{1,0:T(8,128)(2,1)} %param.23) | copy-start | bytes 1966084
  6.5 6.6 %copy-start.7 = (s32[4]{0:T(128)S(1)}, s32[4]{0:T(128)}, u32[]{:S(2)}) copy-start(s32[4]{0:T(128)} %param.13) | copy-start | bytes 52
  6.5 8.0 %copy-start.2 = (bf16[320,320]{1,0:T(8,128)(2,1)S(1)}, bf16[320,320]{1,0:T(8,128)(2,1)}, u32[]{:S(2)}) copy-start(bf16[320,320]{1,0:T(8,128)(2,1)} %param.16) | copy-start | bytes 614404
  6.5 70.5 %all-gather.5.cloned.1.call-start = ((), (), s32[]{:S(2)}) async-start(), calls=%async_computation | async-start | bytes 6553600 | tf_op jit(solution)/shard_map/all_gather | solution.py:88
  8.2 1.4 collective-permute-start
  13.0 155.2 %all-gather.7.cloned.1.call-start = ((), (), s32[]{:S(2)}) async-start(), calls=%async_computation.1 | async-start | bytes 6553600 | tf_op jit(solution)/shard_map/all_gather | solution.py:88
  80.5 6.1 %collective-permute-start.1 = (bf16[1,32,1280]{2,1,0:T(8,128)(2,1)S(1)}, bf16[1,32,1280]{2,1,0:T(8,128)(2,1)S(1)}, u32[]{:S(2)}, u32[]{:S(2)}) collective-permute-start(bf16[1,32,1280]{2,1,0:T(8,128)(2,1)S(1)} %copy.97), channel_id=1, source_target_pairs={{0,1},{1,0},{2,3},{3,2},{4,5},{5,4},{6,7},{7,6},{8,9},{9,8},{10,11... | collective-permute-start | bytes 245768 | tf_op jit(solution)/shard_map/ppermute | solution.py:18
  91.3 2.2 slice-start
  91.6 2.9 %slice-start.1 = ((s8[7372800]{0:T(1024)(128)(4,1)}), s8[3178496]{0:T(1024)(128)(4,1)S(1)}, s32[]{:S(2)}) async-start(s8[7372800]{0:T(1024)(128)(4,1)} %bitcast.120), calls=%async_computation.5 | async-start | bytes 6356992
  91.8 2.7 copy-start.8
  94.5 10.0 %copy-start.3 = (f32[320]{0:T(512)S(1)}, f32[320]{0:T(512)}, u32[]{:S(2)}) copy-start(f32[320]{0:T(512)} %param.17) | copy-start | bytes 3844
  102.8 1.4 collective-permute-start.2
  106.8 119.2 %all-gather.9.cloned.1.call-start = ((), (), s32[]{:S(2)}) async-start(), calls=%async_computation.2 | async-start | bytes 1638400 | tf_op jit(solution)/shard_map/all_gather | solution.py:110
  171.6 6.1 %collective-permute-start.3 = (bf16[1,32,1280]{2,1,0:T(8,128)(2,1)S(1)}, bf16[1,32,1280]{2,1,0:T(8,128)(2,1)S(1)}, u32[]{:S(2)}, u32[]{:S(2)}) collective-permute-start(bf16[1,32,1280]{2,1,0:T(8,128)(2,1)S(1)} %copy.108), channel_id=1, source_target_pairs={{0,1},{1,0},{2,3},{3,2},{4,5},{5,4},{6,7},{7,6},{8,9},{9,8},{10,11... | collective-permute-start | bytes 245768 | tf_op jit(solution)/shard_map/ppermute | solution.py:18
  182.4 2.2 slice-start.2
  182.7 2.9 %slice-start.3 = ((s8[7372800]{0:T(1024)(128)(4,1)}), s8[3178496]{0:T(1024)(128)(4,1)S(1)}, s32[]{:S(2)}) async-start(s8[7372800]{0:T(1024)(128)(4,1)} %bitcast.122), calls=%async_computation.7 | async-start | bytes 6356992
  185.6 8.0 %copy-start.1 = (bf16[16,32,320]{2,1,0:T(8,128)(2,1)S(1)}, bf16[16,32,320]{2,1,0:T(8,128)(2,1)}, u32[]{:S(2)}) copy-start(bf16[16,32,320]{2,1,0:T(8,128)(2,1)} %param.12) | copy-start | bytes 983044
  193.4 2.6 copy-start.4
  193.6 32.3 %copy-start.5 = (bf16[256,1280]{1,0:T(8,128)(2,1)S(1)}, bf16[256,1280]{1,0:T(8,128)(2,1)}, u32[]{:S(2)}) copy-start(bf16[256,1280]{1,0:T(8,128)(2,1)} %param.22) | copy-start | bytes 1966084
  193.6 32.3 %copy-start.6 = (bf16[256,1280]{1,0:T(8,128)(2,1)S(1)}, bf16[256,1280]{1,0:T(8,128)(2,1)}, u32[]{:S(2)}) copy-start(bf16[256,1280]{1,0:T(8,128)(2,1)} %param.21) | copy-start | bytes 1966084
  194.3 1.4 collective-permute-start.4
  197.1 71.5 %all-gather.11.cloned.1.call-start = ((), (), s32[]{:S(2)}) async-start(), calls=%async_computation.3 | async-start | bytes 1310720 | tf_op jit(solution)/shard_map/all_gather | solution.py:129
  228.8 2.0 collective-permute-start.5
Sparse Core Ops, SparseCore 0:
  13.2 63.8 all-gather.4
  106.9 61.2 all-gather.6
  197.2 28.6 all-gather.8
  242.1 26.4 all-gather.10
where the time goes:
time: 278 us
  waiting for transfers between devices  183 us (66%)
  local copies, waits for them, and re-layouts  32 us (12%)
  matrix products  30.8 us (11%)
  other arithmetic  15.9 us (6%)
  between operations  14.3 us (5%)
    all_gather x2, waiting for transfers between devices, convolve(): full = lax.all_gather(active, 'ch', axis=2, tiled=True)  124 us
    all_gather x1, waiting for transfers between devices, body(): lax.all_gather(normed, 'ch', axis=1, tiled=True)  28.8 us
    all_gather x1, waiting for transfers between devices, body(): lax.all_gather(heads_out, 'ch', axis=1, tiled=True)  26.1 us
    conv_general_dilated x2, matrix products, conv_taps(): lax.conv_general_dilated(padded[None], weight, (1, 1), 'VALID', dimension...  15.6 us
    all_gather x2, local copies, waits for them, and re-layouts, convolve(): full = lax.all_gather(active, 'ch', axis=2, tiled=True)  12 us
    select_n x2, other arithmetic, facing_row(): return jnp.where(upper_half, field[-1:], field[:1])  6.06 us
  transfers between devices with their start and end apart: 10, of which 8 were waited for; matrix products, arithmetic and copies ran while one was open for 5% of the time, Pallas kernels for 0%

commit v1 on v0

--- a/solution.py
+++ b/solution.py
@@ -85,7 +85,14 @@
         return jnp.concatenate([above, field, below], axis=0)
 
     def convolve(active, weight):
-        full = lax.all_gather(active, "ch", axis=2, tiled=True)
+        ring = [active]
+        for hop in range(3):
+            ring.append(lax.ppermute(ring[-1], "ch", [(dev, (dev + 1) % 4) for dev in range(4)]))
+        full = jnp.roll(
+            jnp.concatenate(ring[::-1], axis=2),
+            (lax.axis_index("ch") + 1) * ring[0].shape[2],
+            axis=2,
+        )
         partner = swapped(facing_row(full), "row", 0)
         rimmed = attach_rim(full, partner)
         result_conv = conv_taps(pad_columns(rimmed), weight)

time: 278 us -> 201 us (0.72)
  waiting for transfers between devices: 183 us -> 124 us
  local copies, waits for them, and re-layouts: 32 us -> 13.9 us
  other arithmetic: 15.9 us -> 11.4 us
  starting transfers between devices: 2.01 us -> 5.17 us
    all_gather x2 -> x0, waiting for transfers between devices: 124 us -> none  [convolve(): full = lax.all_gather(active, 'ch', axis=2, tiled=True)]
    ppermute x0 -> x6, waiting for transfers between devices: none -> 62.3 us  [convolve(): lax.ppermute(ring[-1], 'ch', [(dev, (dev + 1) % 4) for dev in range(4)])]
    all_gather x2 -> x0, local copies, waits for them, and re-layouts: 12 us -> none  [convolve(): full = lax.all_gather(active, 'ch', axis=2, tiled=True)]
    select_n x2, other arithmetic: 6.06 us -> 0.52 us  [facing_row(): return jnp.where(upper_half, field[-1:], field[:1])]
    concatenate x0 -> x2, local copies, waits for them, and re-layouts: none -> 4.64 us  [convolve(): jnp.concatenate(ring[::-1], axis=2)]
    select_n x6 -> x0, local copies, waits for them, and re-layouts: 4.01 us -> none  [the longest x2 2.54 us: attach_rim(): above = jnp.where(upper_half, empty_row, partner)]
    convert_element_type x2 -> x0, local copies, waits for them, and re-layouts: 3.73 us -> none  [the longest x1 1.96 us: body(): jax.nn.silu(group_norm(hidden_a, norm_gain_b)).astype(jnp.bfloat16)]
    ppermute x0 -> x6, starting transfers between devices: none -> 3.72 us  [convolve(): lax.ppermute(ring[-1], 'ch', [(dev, (dev + 1) % 4) for dev in range(4)])]
  transfers between devices with their start and end apart: 10 -> 14, of which waited for: 8 -> 14; matrix products, arithmetic and copies ran while one was open for 5% -> 2% of each run, Pallas kernels for 0% -> 0%
where the time goes in v1:
time: 201 us
  waiting for transfers between devices  124 us (62%)
  matrix products  31.5 us (16%)
  between operations  14.5 us (7%)
  local copies, waits for them, and re-layouts  13.9 us (7%)
  other arithmetic  11.4 us (6%)
  starting transfers between devices  5.17 us (3%)
    ppermute x6, waiting for transfers between devices, convolve(): lax.ppermute(ring[-1], 'ch', [(dev, (dev + 1) % 4) for dev in range(4)])  62.3 us
    all_gather x1, waiting for transfers between devices, body(): lax.all_gather(normed, 'ch', axis=1, tiled=True)  28.5 us
    all_gather x1, waiting for transfers between devices, body(): lax.all_gather(heads_out, 'ch', axis=1, tiled=True)  26.1 us
    conv_general_dilated x2, matrix products, conv_taps(): lax.conv_general_dilated(padded[None], weight, (1, 1), 'VALID', dimension...  15.6 us
    ppermute x6, waiting for transfers between devices, swapped(): return lax.ppermute(value, axis, pairs)  7.16 us
    dot_general x1, matrix products, body(): jnp.einsum('hqk,khd->qhd', weights, value_heads, preferred_element_type=j...  5.55 us
    sub x1, matrix products, body(): raised = jnp.exp(scores - highest)  4.82 us
    concatenate x2, local copies, waits for them, and re-layouts, convolve(): jnp.concatenate(ring[::-1], axis=2)  4.64 us
  transfers between devices with their start and end apart: 14, of which 14 were waited for; matrix products, arithmetic and copies ran while one was open for 2% of the time, Pallas kernels for 0%

profile of v1, /device:TPU:0, one launch (start us, length us, event | category | flops | bytes accessed | tf_op | source)
XLA Modules:
  0.0 200.5 jit_solution(2828639947794651513)
XLA Ops:
  6.5 1.2 convert_reduce_fusion
  9.9 1.3 fusion.57
  11.2 2.9 %collective-permute-start.1 = (bf16[16,32,320]{2,0,1:T(8,128)(2,1)S(1)}, bf16[16,32,320]{2,0,1:T(8,128)(2,1)S(1)}, u32[]{:S(2)}, u32[]{:S(2)}) collective-permute-start(bf16[16,32,320]{2,0,1:T(8,128)(2,1)S(1)} %fusion.57), channel_id=1, source_target_pairs={{0,8},{8,16},{16,24},{24,0},{1,9},{9,17},{17,25},{25,1},{2,10},{10... | collective-permute-start | bytes 983048 | tf_op jit(solution)/shard_map/ppermute | solution.py:90
  14.1 10.4 %collective-permute-done.1 = bf16[16,32,320]{2,0,1:T(8,128)(2,1)S(1)} collective-permute-done((bf16[16,32,320]{2,0,1:T(8,128)(2,1)S(1)}, bf16[16,32,320]{2,0,1:T(8,128)(2,1)S(1)}, u32[]{:S(2)}, u32[]{:S(2)}) %collective-permute-start.1) | collective-permute-done | bytes 327712 | tf_op jit(solution)/shard_map/ppermute | solution.py:90
  25.3 1.3 fusion.62
  27.2 8.8 %collective-permute-done.2 = bf16[16,32,320]{2,0,1:T(8,128)(2,1)S(1)} collective-permute-done((bf16[16,32,320]{2,0,1:T(8,128)(2,1)S(1)}, bf16[16,32,320]{2,0,1:T(8,128)(2,1)S(1)}, u32[]{:S(2)}, u32[]{:S(2)}) %collective-permute-start.2) | collective-permute-done | bytes 327712 | tf_op jit(solution)/shard_map/ppermute | solution.py:90
  37.3 9.4 %collective-permute-done.3 = bf16[16,32,320]{2,0,1:T(8,128)(2,1)S(1)} collective-permute-done((bf16[16,32,320]{2,0,1:T(8,128)(2,1)S(1)}, bf16[16,32,320]{2,0,1:T(8,128)(2,1)S(1)}, u32[]{:S(2)}, u32[]{:S(2)}) %collective-permute-start.3) | collective-permute-done | bytes 327712 | tf_op jit(solution)/shard_map/ppermute | solution.py:90
  46.6 2.1 %concatenate.27 = bf16[16,32,1280]{2,0,1:T(8,128)(2,1)S(1)} concatenate(bf16[16,32,320]{2,0,1:T(8,128)(2,1)S(1)} %collective-permute-done.3, bf16[16,32,320]{2,0,1:T(8,128)(2,1)S(1)} %collective-permute-done.2, bf16[16,32,320]{2,0,1:T(8,128)(2,1)S(1)} %collective-permute-done.1, bf16[16,32,320]{2,0,1:T(8,128)(2,1)S(1)} %fusion.57), dimensions={2} | concatenate | bytes 2621440 | tf_op jit(solution)/shard_map/concatenate | solution.py:92
  50.3 1.4 collective-permute-done.4
  54.2 1.2 slice-done.1
  55.4 7.8 %select_reduce_fusion.1 = (f32[320]{0:T(512)S(1)}, f32[320]{0:T(512)S(1)}, f32[16,8,5,320]{3,1,2,0:T(8,128)S(1)}) fusion(f32[320]{0:T(512)S(1)} %divide_multiply_fusion, pred[8,5]{0,1:T(8,128)(4,1)S(1)} %copy-done.6, bf16[320,3,3,1280]{3,0,2,1:T(8,128)(2,1)S(1)} %bitcast.121, bf16[18,1,7,2,1280]{4,2,3,0,1:T(8,128)(2,1)S(1)} %slice.69, ...), kind=kOutput, calls=%fused_computation.59 | convolution fusion | flops 4727766016 | bytes 10684200 | tf_op jit(solution)/shard_map/conv_general_dilated | solution.py:28
  65.6 12.1 %collective-permute-done.6 = bf16[16,32,320]{2,0,1:T(8,128)(2,1)S(1)} collective-permute-done((bf16[16,32,320]{2,0,1:T(8,128)(2,1)S(1)}, bf16[16,32,320]{2,0,1:T(8,128)(2,1)S(1)}, u32[]{:S(2)}, u32[]{:S(2)}) %collective-permute-start.6) | collective-permute-done | bytes 327712 | tf_op jit(solution)/shard_map/ppermute | solution.py:90
  77.7 11.2 %collective-permute-done.7 = bf16[16,32,320]{2,0,1:T(8,128)(2,1)S(1)} collective-permute-done((bf16[16,32,320]{2,0,1:T(8,128)(2,1)S(1)}, bf16[16,32,320]{2,0,1:T(8,128)(2,1)S(1)}, u32[]{:S(2)}, u32[]{:S(2)}) %collective-permute-start.7) | collective-permute-done | bytes 327712 | tf_op jit(solution)/shard_map/ppermute | solution.py:90
  88.9 10.5 %collective-permute-done.8 = bf16[16,32,320]{2,0,1:T(8,128)(2,1)} collective-permute-done((bf16[16,32,320]{2,0,1:T(8,128)(2,1)S(1)}, bf16[16,32,320]{2,0,1:T(8,128)(2,1)}, u32[]{:S(2)}, u32[]{:S(2)}) %collective-permute-start.8) | collective-permute-done | bytes 327712 | tf_op jit(solution)/shard_map/ppermute | solution.py:90
  99.4 2.5 %concatenate.30 = bf16[16,32,1280]{2,0,1:T(8,128)(2,1)S(1)} concatenate(bf16[16,32,320]{2,0,1:T(8,128)(2,1)} %collective-permute-done.8, bf16[16,32,320]{2,0,1:T(8,128)(2,1)S(1)} %collective-permute-done.7, bf16[16,32,320]{2,0,1:T(8,128)(2,1)S(1)} %collective-permute-done.6, bf16[16,32,320]{2,0,1:T(8,128)(2,1)S(1)} %multiply_convert_fusion.1), dimensions={2} | concatenate | bytes 2621440 | tf_op jit(solution)/shard_map/concatenate | solution.py:92
  103.4 1.4 collective-permute-done.9
  108.5 7.8 %fusion.37 = f32[16,8,5,320]{3,1,2,0:T(8,128)S(1)} fusion(bf16[320,3,3,1280]{3,0,2,1:T(8,128)(2,1)S(1)} %bitcast.123, bf16[18,1,7,2,1280]{4,2,3,0,1:T(8,128)(2,1)S(1)} %slice.73, bf16[18,1,8,5,1280]{4,2,3,0,1:T(8,128)(2,1)S(1)} %copy.65, pred[8,5]{0,1:T(8,128)(4,1)S(1)} %copy-done.6), kind=kOutput, calls=%fused_computation.49 | convolution fusion | flops 4726538240 | bytes 10680360 | tf_op jit(solution)/shard_map/conv_general_dilated | solution.py:28
  120.1 28.5 %all-gather.3.cloned.1.call-done = bf16[512,1280]{0,1:T(8,128)(2,1)} async-done(((bf16[512,320]{0,1:T(8,128)(2,1)}), bf16[512,1280]{0,1:T(8,128)(2,1)}) %all-gather.3.cloned.1.call-update) | async-done | bytes 1310736 | tf_op jit(solution)/shard_map/all_gather | solution.py:117
  148.6 2.7 %fusion.32 = bf16[512,768]{1,0:T(8,128)(2,1)S(1)} fusion(bf16[512,1280]{0,1:T(8,128)(2,1)} %all-gather.3.cloned.1.call-done, bf16[256,1280]{1,0:T(8,128)(2,1)S(1)} %copy-done.4, bf16[256,1280]{1,0:T(8,128)(2,1)S(1)} %copy-done.5, bf16[256,1280]{1,0:T(8,128)(2,1)} %param.22), kind=kOutput, calls=%fused_computation.42 | convolution fusion | flops 1012924416 | bytes 4063232 | tf_op jit(solution)/shard_map/dot_general | solution.py:22
  151.6 1.7 collective-permute-done.11
  154.0 4.8 %fusion.83 = (f32[4,512]{1,0:T(4,128)S(1)}, f32[4,512,1024]{2,1,0:T(8,128)}) fusion(bf16[512,4,64]{0,2,1:T(8,128)(2,1)S(1)} %bitcast.106, bf16[1024,4,64]{0,2,1:T(8,128)(2,1)S(1)} %bitcast.104), kind=kOutput, calls=%fused_computation.124 | convolution fusion | flops 274727936 | bytes 9183232 | tf_op jit(solution)/shard_map/sub | solution.py:131
  158.8 5.5 %fusion.46 = bf16[4,64,512]{2,1,0:T(8,128)(2,1)} fusion(bf16[1024,4,64]{0,2,1:T(8,128)(2,1)S(1)} %bitcast.105, f32[4,512,1024]{2,1,0:T(8,128)} %get-tuple-element.24, f32[4,512]{1,0:T(4,128)S(1)} %get-tuple-element.23), kind=kOutput, calls=%fused_computation.55 | convolution fusion | flops 272760832 | bytes 9183232 | tf_op jit(solution)/shard_map/hqk,khd->qhd/dot_general | solution.py:133
  164.9 26.1 %all-gather.5.cloned.1.call-done = bf16[512,1024]{0,1:T(8,128)(2,1)} async-done(((bf16[512,256]{0,1:T(8,128)(2,1)}), bf16[512,1024]{0,1:T(8,128)(2,1)}) %all-gather.5.cloned.1.call-update) | async-done | bytes 1048592 | tf_op jit(solution)/shard_map/all_gather | solution.py:136
  191.0 1.7 fusion.45
  (113 shorter events, 21.6 us)
Async XLA Ops:
  6.5 184.5 %copy-start = (bf16[320,1024]{1,0:T(8,128)(2,1)S(1)}, bf16[320,1024]{1,0:T(8,128)(2,1)}, u32[]{:S(2)}) copy-start(bf16[320,1024]{1,0:T(8,128)(2,1)} %param.25) | copy-start | bytes 1966084
  6.5 142.0 %all-gather.3.cloned.1.call-start = ((), (), s32[]{:S(2)}) async-start(), calls=%async_computation | async-start | bytes 1638400 | tf_op jit(solution)/shard_map/all_gather | solution.py:117
  8.2 1.4 collective-permute-start
  11.2 13.3 %collective-permute-start.1 = (bf16[16,32,320]{2,0,1:T(8,128)(2,1)S(1)}, bf16[16,32,320]{2,0,1:T(8,128)(2,1)S(1)}, u32[]{:S(2)}, u32[]{:S(2)}) collective-permute-start(bf16[16,32,320]{2,0,1:T(8,128)(2,1)S(1)} %fusion.57), channel_id=1, source_target_pairs={{0,8},{8,16},{16,24},{24,0},{1,9},{9,17},{17,25},{25,1},{2,10},{10... | collective-permute-start | bytes 983048 | tf_op jit(solution)/shard_map/ppermute | solution.py:90
  24.5 11.5 %collective-permute-start.2 = (bf16[16,32,320]{2,0,1:T(8,128)(2,1)S(1)}, bf16[16,32,320]{2,0,1:T(8,128)(2,1)S(1)}, u32[]{:S(2)}, u32[]{:S(2)}) collective-permute-start(bf16[16,32,320]{2,0,1:T(8,128)(2,1)S(1)} %collective-permute-done.1), channel_id=1, source_target_pairs={{0,8},{8,16},{16,24},{24,0},{1,9},{9,17},{17,25},{25,1},{2,10},{10... | collective-permute-start | bytes 983048 | tf_op jit(solution)/shard_map/ppermute | solution.py:90
  36.0 10.6 %collective-permute-start.3 = (bf16[16,32,320]{2,0,1:T(8,128)(2,1)S(1)}, bf16[16,32,320]{2,0,1:T(8,128)(2,1)S(1)}, u32[]{:S(2)}, u32[]{:S(2)}) collective-permute-start(bf16[16,32,320]{2,0,1:T(8,128)(2,1)S(1)} %collective-permute-done.2), channel_id=1, source_target_pairs={{0,8},{8,16},{16,24},{24,0},{1,9},{9,17},{17,25},{25,1},{2,10},{10... | collective-permute-start | bytes 983048 | tf_op jit(solution)/shard_map/ppermute | solution.py:90
  50.3 1.5 collective-permute-start.4
  52.0 2.2 %slice-start = ((s8[7372800]{0:T(1024)(128)(4,1)}), s8[4194304]{0:T(1024)(128)(4,1)S(1)}, s32[]{:S(2)}) async-start(s8[7372800]{0:T(1024)(128)(4,1)} %bitcast.120), calls=%async_computation.2 | async-start | bytes 8388608
  53.2 2.2 %slice-start.1 = ((s8[7372800]{0:T(1024)(128)(4,1)}), s8[3178496]{0:T(1024)(128)(4,1)S(1)}, s32[]{:S(2)}) async-start(s8[7372800]{0:T(1024)(128)(4,1)} %bitcast.120), calls=%async_computation.3 | async-start | bytes 6356992
  55.4 9.8 %copy-start.2 = (f32[320]{0:T(512)S(1)}, f32[320]{0:T(512)}, u32[]{:S(2)}) copy-start(f32[320]{0:T(512)} %param.19) | copy-start | bytes 3844
  63.7 1.2 collective-permute-start.5
  65.5 12.1 %collective-permute-start.6 = (bf16[16,32,320]{2,0,1:T(8,128)(2,1)S(1)}, bf16[16,32,320]{2,0,1:T(8,128)(2,1)S(1)}, u32[]{:S(2)}, u32[]{:S(2)}) collective-permute-start(bf16[16,32,320]{2,0,1:T(8,128)(2,1)S(1)} %multiply_convert_fusion.1), channel_id=1, source_target_pairs={{0,8},{8,16},{16,24},{24,0},{1,9},{9,17},{17,25},{25,1},{2,10},{10... | collective-permute-start | bytes 983048 | tf_op jit(solution)/shard_map/ppermute | solution.py:90
  77.7 11.2 %collective-permute-start.7 = (bf16[16,32,320]{2,0,1:T(8,128)(2,1)S(1)}, bf16[16,32,320]{2,0,1:T(8,128)(2,1)S(1)}, u32[]{:S(2)}, u32[]{:S(2)}) collective-permute-start(bf16[16,32,320]{2,0,1:T(8,128)(2,1)S(1)} %collective-permute-done.6), channel_id=1, source_target_pairs={{0,8},{8,16},{16,24},{24,0},{1,9},{9,17},{17,25},{25,1},{2,10},{10... | collective-permute-start | bytes 983048 | tf_op jit(solution)/shard_map/ppermute | solution.py:90
  88.9 10.5 %collective-permute-start.8 = (bf16[16,32,320]{2,0,1:T(8,128)(2,1)S(1)}, bf16[16,32,320]{2,0,1:T(8,128)(2,1)}, u32[]{:S(2)}, u32[]{:S(2)}) collective-permute-start(bf16[16,32,320]{2,0,1:T(8,128)(2,1)S(1)} %collective-permute-done.7), channel_id=1, source_target_pairs={{0,8},{8,16},{16,24},{24,0},{1,9},{9,17},{17,25},{25,1},{2,10},{10... | collective-permute-start | bytes 983048 | tf_op jit(solution)/shard_map/ppermute | solution.py:90
  103.3 1.5 collective-permute-start.9
  105.1 2.2 %slice-start.2 = ((s8[7372800]{0:T(1024)(128)(4,1)}), s8[4194304]{0:T(1024)(128)(4,1)S(1)}, s32[]{:S(2)}) async-start(s8[7372800]{0:T(1024)(128)(4,1)} %bitcast.122), calls=%async_computation.4 | async-start | bytes 8388608
  106.3 2.2 %slice-start.3 = ((s8[7372800]{0:T(1024)(128)(4,1)}), s8[3178496]{0:T(1024)(128)(4,1)S(1)}, s32[]{:S(2)}) async-start(s8[7372800]{0:T(1024)(128)(4,1)} %bitcast.122), calls=%async_computation.5 | async-start | bytes 6356992
  108.5 8.0 %copy-start.1 = (bf16[16,32,320]{2,1,0:T(8,128)(2,1)S(1)}, bf16[16,32,320]{2,1,0:T(8,128)(2,1)}, u32[]{:S(2)}) copy-start(bf16[16,32,320]{2,1,0:T(8,128)(2,1)} %param.14) | copy-start | bytes 983044
  116.3 2.4 %copy-start.3 = (f32[320]{0:T(512)S(1)}, f32[320]{0:T(512)}, u32[]{:S(2)}) copy-start(f32[320]{0:T(512)} %param.21) | copy-start | bytes 3844
  116.5 32.1 %copy-start.4 = (bf16[256,1280]{1,0:T(8,128)(2,1)S(1)}, bf16[256,1280]{1,0:T(8,128)(2,1)}, u32[]{:S(2)}) copy-start(bf16[256,1280]{1,0:T(8,128)(2,1)} %param.24) | copy-start | bytes 1966084
  116.5 32.1 %copy-start.5 = (bf16[256,1280]{1,0:T(8,128)(2,1)S(1)}, bf16[256,1280]{1,0:T(8,128)(2,1)}, u32[]{:S(2)}) copy-start(bf16[256,1280]{1,0:T(8,128)(2,1)} %param.23) | copy-start | bytes 1966084
  117.1 1.2 collective-permute-start.10
  119.8 71.2 %all-gather.5.cloned.1.call-start = ((), (), s32[]{:S(2)}) async-start(), calls=%async_computation.1 | async-start | bytes 1310720 | tf_op jit(solution)/shard_map/all_gather | solution.py:136
  151.4 2.0 collective-permute-start.11
  (1 other events, 2.0 us)
Sparse Core Ops, SparseCore 0:
  119.9 28.5 all-gather.2
  164.5 26.4 all-gather.4
